TPU v7x, 32 devices: a whole 2x2x4 slice. The times are simulated.
32 devices in a mesh: gx: 8 (over y, x, core), gy: 4 (over z).
Axes of the slice: x: 2, y: 2, z: 4, core: 2. Of those that a mesh axis runs over, the one named last changes fastest.
Arguments:
- velocity: float32 [3, 1, 384, 1024], P(None, None, 'gy', 'gx'), may hold values from -6 to 6
- block_inverse: float32 [384, 96], P('gy'), may hold values from -1.6 to 1.6, as said below
- lower_map: float32 [384, 96], P('gy'), may hold values from -1 to 1
- upper_map: float32 [384, 96], P('gy'), may hold values from -1 to 1
Outputs:
- new_velocity: float32 [3, 1, 384, 2048], P(None, None, 'gy', 'gx')
Inputs may be any that keep to these rules, and one draw needn't show every extreme that they name: `block_inverse`: entries of the given block inverses.
All inputs are finite; a program needn't handle non-finite values.
Results may differ from a plain program's by a relative error of at most 0.00012.
Values sent between devices are 32-bit elements; how exact they have to be, the bound alone decides.
A program may use at most 64 MiB of HBM per device.

v0:
```python
import math
import jax
import jax.numpy as jnp
from jax import lax
from jax.sharding import PartitionSpec as P

courant = 0.8


def from_partner(shard, axis, bit):
    return lax.ppermute(shard, axis, [(i, i ^ 1 << bit) for i in range(lax.axis_size(axis))])


def reversed_position(position, levels):
    result = jnp.zeros((), jnp.int32)
    for digit_place in range(levels):
        result = result + (position >> digit_place & 1) * (1 << levels - 1 - digit_place)
    return result


def advance(matrix, state):
    return jnp.einsum("ab,spbw->spaw", matrix, state, precision=lax.Precision.HIGHEST)


def local_transform(paired, leading, count_gx, total_x):
    local_x = paired.shape[-1] // 2
    cells = jnp.arange(local_x, dtype=jnp.int32)
    wavenumbers = leading + count_gx * cells
    phases = cells[:, None] * wavenumbers[None, :] % total_x
    angles = 2.0 * math.pi / total_x * phases.astype(jnp.float32)
    cosine = jnp.cos(angles)
    sine_table = jnp.sin(angles)
    transform_matrix = jnp.concatenate(
        [jnp.concatenate([cosine, -sine_table], 1), jnp.concatenate([sine_table, cosine], 1)], 0
    )
    product = jnp.dot(
        paired,
        transform_matrix,
        precision=lax.Precision.HIGHEST,
        preferred_element_type=jnp.float32,
    )
    return product * (1.0 / math.sqrt(total_x))


def local_sweeps(lower_blocks, upper_blocks, loads):

    def step_once(state_prev, inputs):
        fresh = inputs[1] + advance(inputs[0], state_prev)
        return (fresh, fresh)

    start_state = jnp.zeros(loads.shape[1:], jnp.float32)
    unused, sweeps = lax.scan(step_once, start_state, (lower_blocks, loads))
    unused, solved = lax.scan(step_once, start_state, (upper_blocks, sweeps), reverse=True)
    return solved


def shards(velocity, block_inverse, lower_map, upper_map):
    fluxes = velocity[0:1] * velocity
    fields = jnp.concatenate([velocity, fluxes], 0)
    planes_here = fields.shape[1]
    rows_here = fields.shape[2]
    local_x = fields.shape[3]
    count_gx = lax.axis_size("gx")
    levels = count_gx.bit_length() - 1
    position = lax.axis_index("gx")
    total_x = local_x * count_gx
    current = jnp.stack([fields, jnp.zeros_like(fields)])
    for digit_place in reversed(range(levels)):
        half_span = 1 << digit_place
        if digit_place == levels - 1:
            real_partner = from_partner(fields, "gx", digit_place)
            partner = jnp.stack([real_partner, jnp.zeros_like(real_partner)])
        else:
            partner = from_partner(current, "gx", digit_place)
        is_upper = position >> digit_place & 1 == 1
        offset = (position & half_span - 1).astype(jnp.float32)
        angles = offset * (-math.pi / half_span)
        cosine = jnp.cos(angles)
        sine_value = jnp.sin(angles)
        diff_real = partner[0] - current[0]
        diff_imag = partner[1] - current[1]
        turned = jnp.stack(
            [
                diff_real * cosine - diff_imag * sine_value,
                diff_real * sine_value + diff_imag * cosine,
            ]
        )
        current = jnp.where(is_upper, turned, current + partner)
    paired = jnp.concatenate([current[0], current[1]], -1)
    leading = reversed_position(position, levels)
    spectra = local_transform(paired, leading, count_gx, total_x)
    velocity_modes = spectra[:3]
    flux_modes = spectra[3:]
    wavenumbers = leading + count_gx * jnp.arange(local_x, dtype=jnp.int32)
    signed = jnp.where(wavenumbers < total_x // 2, wavenumbers, wavenumbers - total_x)
    factor = courant * signed.astype(jnp.float32) / (total_x // 2)
    side_real = velocity_modes[..., :local_x] + factor * flux_modes[..., local_x:]
    side_imag = velocity_modes[..., local_x:] - factor * flux_modes[..., :local_x]
    right_side = jnp.concatenate([side_real, side_imag], -1)
    loads = advance(block_inverse, right_side)
    count_gy = lax.axis_size("gy")
    column_total = loads.shape[-1]
    column_count = column_total // count_gy
    lowers, uppers = (
        lax.all_gather(lower_map, "gy", axis=0, tiled=True),
        lax.all_gather(upper_map, "gy", axis=0, tiled=True),
    )
    lower_blocks = lowers.reshape(count_gy, rows_here, rows_here)
    upper_blocks = uppers.reshape(count_gy, rows_here, rows_here)
    grouped = loads.reshape(3, planes_here, rows_here, count_gy, column_count)
    profiles = lax.all_to_all(grouped, "gy", split_axis=3, concat_axis=2, tiled=True)
    items = profiles.shape[0]
    blocked = profiles.reshape(items, planes_here, count_gy, rows_here, column_count)
    blocked = jnp.moveaxis(blocked, 2, 0)
    solved_blocks = local_sweeps(lower_blocks, upper_blocks, blocked)
    whole = jnp.moveaxis(solved_blocks, 0, 2).reshape(
        items, planes_here, count_gy * rows_here, 1, column_count
    )
    finished = lax.all_to_all(whole, "gy", split_axis=2, concat_axis=3, tiled=True)
    solved = finished.reshape(3, planes_here, rows_here, column_total)
    return solved


def solution(mesh):
    return jax.shard_map(
        shards,
        mesh=mesh,
        in_specs=(P(None, None, "gy", "gx"), P("gy", None), P("gy", None), P("gy", None)),
        out_specs=P(None, None, "gy", "gx"),
        check_vma=False,
    )
```

profile of v0, /device:TPU:0, one launch (start us, length us, event | category | flops | bytes accessed | tf_op | source)
XLA Modules:
  0.0 91.6 jit_solution(16802690939830432598)
XLA Ops:
  0.0 0.0 copy-start
  0.0 0.8 slice_bitcast_fusion.2
  0.8 1.0 %broadcast_multiply_fusion = f32[3,1,96,128]{3,2,0,1:T(8,128)S(1)} fusion(f32[96,128]{1,0:T(8,128)S(1)} %slice_bitcast_fusion.2, f32[3,1,96,128]{3,2,1,0:T(8,128)} %param.8), kind=kLoop, calls=%fused_computation.53 | loop fusion | flops 36864 | bytes 344064 | tf_op jit(solution)/shard_map/mul | solution.py:58
  1.8 0.0 copy-done.1
  1.9 3.1 %collective-permute-start = (f32[6,1,96,128]{3,2,0,1:T(8,128)S(1)}, f32[6,1,96,128]{3,2,0,1:T(8,128)S(1)}, u32[]{:S(2)}, u32[]{:S(2)}) collective-permute-start(f32[6,1,96,128]{3,2,0,1:T(8,128)S(1)} %pad_maximum_fusion), channel_id=1, source_target_pairs={{0,16},{4,20},{8,24},{12,28},{16,0},{20,4},{24,8},{28,12},{1,17},{... | collective-permute-start | bytes 884744 | tf_op jit(solution)/shard_map/ppermute | solution.py:11
  5.1 6.8 %collective-permute-done = f32[6,1,96,128]{3,2,0,1:T(8,128)S(1)} collective-permute-done((f32[6,1,96,128]{3,2,0,1:T(8,128)S(1)}, f32[6,1,96,128]{3,2,0,1:T(8,128)S(1)}, u32[]{:S(2)}, u32[]{:S(2)}) %collective-permute-start) | collective-permute-done | bytes 294944 | tf_op jit(solution)/shard_map/ppermute | solution.py:11
  11.9 0.1 subtract_bitcast_fusion
  12.0 0.1 maximum_select_fusion
  12.1 1.8 %collective-permute-start.1 = (f32[2,6,1,96,128]{4,3,1,2,0:T(8,128)S(1)}, f32[2,6,1,96,128]{4,3,1,2,0:T(8,128)S(1)}, u32[]{:S(2)}, u32[]{:S(2)}) collective-permute-start(f32[2,6,1,96,128]{4,3,1,2,0:T(8,128)S(1)} %maximum_select_fusion), channel_id=1, source_target_pairs={{0,8},{4,12},{8,0},{12,4},{16,24},{20,28},{24,16},{28,20},{1,9},{5... | collective-permute-start | bytes 1769480 | tf_op jit(solution)/shard_map/ppermute | solution.py:11
  14.0 12.6 %collective-permute-done.1 = f32[2,6,1,96,128]{4,3,1,2,0:T(8,128)S(1)} collective-permute-done((f32[2,6,1,96,128]{4,3,1,2,0:T(8,128)S(1)}, f32[2,6,1,96,128]{4,3,1,2,0:T(8,128)S(1)}, u32[]{:S(2)}, u32[]{:S(2)}) %collective-permute-start.1) | collective-permute-done | bytes 589856 | tf_op jit(solution)/shard_map/ppermute | solution.py:11
  26.6 0.1 multiply_subtract_fusion.1
  26.7 0.1 maximum_select_fusion.1
  26.9 0.1 collective-permute-start.2
  27.0 0.3 fusion.30
  27.3 1.7 %collective-permute-done.2 = f32[2,6,1,96,128]{4,3,1,2,0:T(8,128)S(1)} collective-permute-done((f32[2,6,1,96,128]{4,3,1,2,0:T(8,128)S(1)}, f32[2,6,1,96,128]{4,3,1,2,0:T(8,128)S(1)}, u32[]{:S(2)}, u32[]{:S(2)}) %collective-permute-start.2) | collective-permute-done | bytes 589856 | tf_op jit(solution)/shard_map/ppermute | solution.py:11
  29.0 0.1 multiply_subtract_fusion
  29.0 0.1 maximum_select_fusion.2
  29.2 0.6 fusion.8
  29.9 0.4 convolution_bitcast_fusion
  30.3 0.2 copy.27
  30.5 0.8 copy.28
  31.2 4.9 %all-to-all-start = ((f32[3,1,96,4,64]{2,4,0,1,3:T(8,128)}), f32[3,1,96,4,64]{2,4,0,1,3:T(8,128)S(1)}, u32[]{:S(2)}, u32[]{:S(2)}) async-start(f32[3,1,96,4,64]{2,4,0,1,3:T(8,128)} %copy.28), calls=%async_computation | async-start | bytes 786432 | tf_op jit(solution)/shard_map/all_to_all | solution.py:111
  36.2 0.0 copy-done.2
  36.2 19.4 %all_gather.6 = f32[384,96]{1,0:T(8,128)S(1)} all-gather(f32[96,96]{1,0:T(8,128)S(1)} %copy-done.2), channel_id=1, replica_groups=mesh['gx'=8,'gy'=4] {'gy'}, dimensions={0}, use_global_device_ids=true | all-gather | bytes 184320 | tf_op jit(solution)/shard_map/all_gather | solution.py:105
  55.6 0.0 copy-done.3
  55.6 13.6 %all_gather.7 = f32[384,96]{1,0:T(8,128)S(1)} all-gather(f32[96,96]{1,0:T(8,128)S(1)} %copy-done.3), channel_id=1, replica_groups=mesh['gx'=8,'gy'=4] {'gy'}, dimensions={0}, use_global_device_ids=true | all-gather | bytes 184320 | tf_op jit(solution)/shard_map/all_gather | solution.py:106
  69.2 0.0 all-to-all-done
  69.2 1.3 %while.30 = (s32[]{:T(128)}, f32[3,1,96,64]{2,3,0,1:T(8,128)S(1)}, f32[4,3,1,96,64]{3,4,1,2,0:T(8,128)S(1)}, f32[4,3,1,96,64]{3,4,1,2,0:T(8,128)S(1)}, f32[4,96,96]{2,1,0:T(8,128)S(1)}, /*index=5*/s32[]{:T(128)}, s32[]{:T(128)}) while((s32[]{:T(128)}, f32[3,1,96,64]{2,3,0,1:T(8,128)S(1)}, f32[4,3,1,96,64]{3,4,1,2,0:T(8,128)S(1)}, ...), condition=%wide.region_1.2_spmd.clone, body=%wide.region_0.1_spmd.clone.sunk | while | flops 21270532 | bytes 786527 | solution.py:52
  69.3 0.2 fusion.46
  69.6 0.3 fusion.46
  69.9 0.3 fusion.46
  70.2 0.3 fusion.46
  70.6 1.3 %while.31 = (s32[]{:T(128)}, f32[3,1,96,64]{2,3,0,1:T(8,128)S(1)}, f32[4,3,1,96,64]{3,4,1,2,0:T(8,128)S(1)}, f32[4,3,1,96,64]{3,4,1,2,0:T(8,128)S(1)}, f32[4,96,...) while((s32[]{:T(128)}, f32[3,1,96,64]{2,3,0,1:T(8,128)S(1)}, ...), condition=%wide.region_3.4_spmd.clone, body=%wide.region_2.3_spmd.clone.sunk | while | flops 21270532 | bytes 786547 | solution.py:53
  70.6 0.2 fusion.49
  70.9 0.3 fusion.49
  71.3 0.2 fusion.49
  71.6 0.3 fusion.49
  71.9 0.3 copy.35
  72.2 0.7 reshape.122
  73.0 0.5 broadcast.111
  73.5 2.6 %reduce = f32[384,3,64]{2,1,0:T(4,128)S(1)} reduce(f32[384,3,1,1,64]{4,3,2,1,0:T(1,128)S(1)} %bitcast.125, f32[]{:T(128)} %broadcast.111), dimensions={2,3}, to_apply=%bitcast.93.reduce_sub_computation | reduce | bytes 589828
  76.1 0.6 reshape.123
  76.7 10.8 %all_to_all.30 = f32[4,1,18432]{2,1,0:T(1,128)S(1)} all-to-all(f32[4,1,18432]{2,1,0:T(1,128)S(1)} %reshape.123), channel_id=1, replica_groups=mesh['gx'=8,'gy'=4] {'gy'}, dimensions={0} | all-to-all | bytes 589824 | tf_op jit(solution)/shard_map/all_to_all | solution.py:119
  87.5 1.5 %reduce.1 = f32[4,18432]{1,0:T(4,128)S(1)} reduce(f32[4,1,18432]{2,1,0:T(1,128)S(1)} %all_to_all.30, f32[]{:T(128)} %broadcast.111), dimensions={1}, to_apply=%all_to_all.25.reduce_sub_computation | reduce | bytes 589828 | tf_op jit(solution)/shard_map/all_to_all | solution.py:119
  88.9 0.7 reshape.124
  89.7 0.8 copy.32
  90.5 0.3 all_to_all.26
  90.8 0.9 copy.34
  (30 shorter events, 0.5 us)
Async XLA Ops:
  0.0 29.9 %copy-start = (f32[96,96]{1,0:T(8,128)S(1)}, f32[96,96]{1,0:T(8,128)}, u32[]{:S(2)}) copy-start(f32[96,96]{1,0:T(8,128)} %param.9) | copy-start | bytes 110596
  0.8 1.0 %copy-start.1 = (f32[3,1,96,128]{3,2,1,0:T(8,128)S(1)}, f32[3,1,96,128]{3,2,1,0:T(8,128)}, u32[]{:S(2)}) copy-start(f32[3,1,96,128]{3,2,1,0:T(8,128)} %param.8) | copy-start | bytes 442372
  1.9 10.1 %collective-permute-start = (f32[6,1,96,128]{3,2,0,1:T(8,128)S(1)}, f32[6,1,96,128]{3,2,0,1:T(8,128)S(1)}, u32[]{:S(2)}, u32[]{:S(2)}) collective-permute-start(f32[6,1,96,128]{3,2,0,1:T(8,128)S(1)} %pad_maximum_fusion), channel_id=1, source_target_pairs={{0,16},{4,20},{8,24},{12,28},{16,0},{20,4},{24,8},{28,12},{1,17},{... | collective-permute-start | bytes 884744 | tf_op jit(solution)/shard_map/ppermute | solution.py:11
  12.1 14.6 %collective-permute-start.1 = (f32[2,6,1,96,128]{4,3,1,2,0:T(8,128)S(1)}, f32[2,6,1,96,128]{4,3,1,2,0:T(8,128)S(1)}, u32[]{:S(2)}, u32[]{:S(2)}) collective-permute-start(f32[2,6,1,96,128]{4,3,1,2,0:T(8,128)S(1)} %maximum_select_fusion), channel_id=1, source_target_pairs={{0,8},{4,12},{8,0},{12,4},{16,24},{20,28},{24,16},{28,20},{1,9},{5... | collective-permute-start | bytes 1769480 | tf_op jit(solution)/shard_map/ppermute | solution.py:11
  26.9 2.1 %collective-permute-start.2 = (f32[2,6,1,96,128]{4,3,1,2,0:T(8,128)S(1)}, f32[2,6,1,96,128]{4,3,1,2,0:T(8,128)S(1)}, u32[]{:S(2)}, u32[]{:S(2)}) collective-permute-start(f32[2,6,1,96,128]{4,3,1,2,0:T(8,128)S(1)} %maximum_select_fusion.1), channel_id=1, source_target_pairs={{0,4},{4,0},{8,12},{12,8},{16,20},{20,16},{24,28},{28,24},{1,5},{5... | collective-permute-start | bytes 1769480 | tf_op jit(solution)/shard_map/ppermute | solution.py:11
  31.2 4.9 %copy-start.2 = (f32[96,96]{1,0:T(8,128)S(1)}, f32[96,96]{1,0:T(8,128)}, u32[]{:S(2)}) copy-start(f32[96,96]{1,0:T(8,128)} %param.10) | copy-start | bytes 110596
  31.2 37.9 %all-to-all-start = ((f32[3,1,96,4,64]{2,4,0,1,3:T(8,128)}), f32[3,1,96,4,64]{2,4,0,1,3:T(8,128)S(1)}, u32[]{:S(2)}, u32[]{:S(2)}) async-start(f32[3,1,96,4,64]{2,4,0,1,3:T(8,128)} %copy.28), calls=%async_computation | async-start | bytes 786432 | tf_op jit(solution)/shard_map/all_to_all | solution.py:111
  36.2 19.4 %copy-start.3 = (f32[96,96]{1,0:T(8,128)S(1)}, f32[96,96]{1,0:T(8,128)}, u32[]{:S(2)}) copy-start(f32[96,96]{1,0:T(8,128)} %param.11) | copy-start | bytes 110596
where the time goes:
time: 92 us; the launch traced here: 91.6 us
  blocking collectives  43.8 us (48%)
  waiting for transfers between devices  21.1 us (23%)
  starting transfers between devices  9.85 us (11%)
  local copies, waits for them, and re-layouts  6.69 us (7%)
  other arithmetic  6.21 us (7%)
  matrix products  3.06 us (3%)
    ppermute x3, waiting for transfers between devices, from_partner(): lax.ppermute(shard, axis, [(i, i ^ 1 << bit) for i in range(lax.axis_size...  21.1 us
    all_gather x1, blocking collectives, shards(): lax.all_gather(lower_map, 'gy', axis=0, tiled=True)  19.4 us
    all_gather x1, blocking collectives, shards(): lax.all_gather(upper_map, 'gy', axis=0, tiled=True)  13.6 us
    all_to_all x1, blocking collectives, shards(): lax.all_to_all(whole, 'gy', split_axis=2, concat_axis=3, tiled=True)  10.8 us
    all_to_all x1, starting transfers between devices, shards(): lax.all_to_all(grouped, 'gy', split_axis=3, concat_axis=2, tiled=True)  4.94 us
    ppermute x3, starting transfers between devices, from_partner(): lax.ppermute(shard, axis, [(i, i ^ 1 << bit) for i in range(lax.axis_size...  4.91 us
    unnamed x3, other arithmetic  2.57 us
    while x8, matrix products  2.02 us
  transfers between devices with their start and end apart: 4, of which 3 were waited for; matrix products, arithmetic and copies ran while one was open for 0% of the time, Pallas kernels for 0%

commit v1 on v0

--- a/solution.py
+++ b/solution.py
@@ -3,6 +3,7 @@
 import jax.numpy as jnp
 from jax import lax
 from jax.sharding import PartitionSpec as P
+from jax.lax import axis_index, axis_size, ppermute
 
 courant = 0.8
 
@@ -108,7 +109,21 @@
     lower_blocks = lowers.reshape(count_gy, rows_here, rows_here)
     upper_blocks = uppers.reshape(count_gy, rows_here, rows_here)
     grouped = loads.reshape(3, planes_here, rows_here, count_gy, column_count)
-    profiles = lax.all_to_all(grouped, "gy", split_axis=3, concat_axis=2, tiled=True)
+    opened = axis_size("gy")
+    field_out = axis_index("gy")
+    local_next, block_last = (opened, field_out)
+    x_new = grouped.shape[3] // local_next
+    known = jnp.roll(grouped, -block_last * x_new, 3)
+    kept_arr = lax.slice_in_dim(known, 0, x_new, axis=3)
+    buffer = [kept_arr]
+    for k0 in [*range(1, local_next)]:
+        now = lax.slice_in_dim(known, k0 * x_new, (k0 + 1) * x_new, axis=3)
+        z2 = ppermute(
+            now, axis_name="gy", perm=[(c, (c + k0) % local_next) for c in range(local_next)]
+        )
+        buffer.append(z2)
+    e_next = jnp.concatenate(buffer[::-1], 2)
+    profiles = jnp.roll(e_next, (block_last + 1) * buffer[0].shape[2], 2)
     items = profiles.shape[0]
     blocked = profiles.reshape(items, planes_here, count_gy, rows_here, column_count)
     blocked = jnp.moveaxis(blocked, 2, 0)

time: 92 us -> 89.1 us (0.968)
  blocking collectives: 43.8 us -> 40.8 us
    all_to_all x1 -> x0, starting transfers between devices: 4.94 us -> none  [shards(): lax.all_to_all(grouped, 'gy', split_axis=3, concat_axis=2, tiled=True)]
    ppermute x0 -> x3, starting transfers between devices: none -> 4.61 us  [shards(): ppermute(now, axis_name='gy', perm=[(c, (c + k0) % local_next) for c in r...]
    all_gather x1, blocking collectives: 19.4 us -> 16.9 us  [shards(): lax.all_gather(lower_map, 'gy', axis=0, tiled=True)]
  transfers between devices with their start and end apart: 4 -> 6, of which waited for: 3 -> 3; matrix products, arithmetic and copies ran while one was open for 0% -> 0% of each run, Pallas kernels for 0% -> 0%
where the time goes in v1:
time: 89.1 us; the launch traced here: 88.8 us
  blocking collectives  40.8 us (46%)
  waiting for transfers between devices  21.1 us (24%)
  starting transfers between devices  9.52 us (11%)
  local copies, waits for them, and re-layouts  7.02 us (8%)
  other arithmetic  6.28 us (7%)
  matrix products  3.07 us (3%)
    ppermute x3, waiting for transfers between devices, from_partner(): lax.ppermute(shard, axis, [(i, i ^ 1 << bit) for i in range(lax.axis_size...  21.1 us
    all_gather x1, blocking collectives, shards(): lax.all_gather(lower_map, 'gy', axis=0, tiled=True)  16.9 us
    all_gather x1, blocking collectives, shards(): lax.all_gather(upper_map, 'gy', axis=0, tiled=True)  13.6 us
    all_to_all x1, blocking collectives, shards(): lax.all_to_all(whole, 'gy', split_axis=2, concat_axis=3, tiled=True)  10.3 us
    ppermute x3, starting transfers between devices, from_partner(): lax.ppermute(shard, axis, [(i, i ^ 1 << bit) for i in range(lax.axis_size...  4.91 us
    ppermute x3, starting transfers between devices, shards(): ppermute(now, axis_name='gy', perm=[(c, (c + k0) % local_next) for c in r...  4.61 us
    unnamed x3, other arithmetic  2.57 us
    while x8, matrix products  2.02 us
  transfers between devices with their start and end apart: 6, of which 3 were waited for; matrix products, arithmetic and copies ran while one was open for 0% of the time, Pallas kernels for 0%

profile of v1, /device:TPU:0, one launch (start us, length us, event | category | flops | bytes accessed | tf_op | source)
XLA Modules:
  0.0 88.8 jit_solution(3186775546613749043)
XLA Ops:
  0.0 0.8 slice_bitcast_fusion.2
  0.8 1.0 %broadcast_multiply_fusion = f32[3,1,96,128]{3,2,0,1:T(8,128)S(1)} fusion(f32[96,128]{1,0:T(8,128)S(1)} %slice_bitcast_fusion.2, f32[3,1,96,128]{3,2,1,0:T(8,128)} %param.8), kind=kLoop, calls=%fused_computation.56 | loop fusion | flops 36864 | bytes 344064 | tf_op jit(solution)/shard_map/mul | solution.py:59
  1.9 3.1 %collective-permute-start = (f32[6,1,96,128]{3,2,0,1:T(8,128)S(1)}, f32[6,1,96,128]{3,2,0,1:T(8,128)S(1)}, u32[]{:S(2)}, u32[]{:S(2)}) collective-permute-start(f32[6,1,96,128]{3,2,0,1:T(8,128)S(1)} %pad_maximum_fusion), channel_id=1, source_target_pairs={{0,16},{4,20},{8,24},{12,28},{16,0},{20,4},{24,8},{28,12},{1,17},{... | collective-permute-start | bytes 884744 | tf_op jit(solution)/shard_map/ppermute | solution.py:12
  5.1 6.8 %collective-permute-done = f32[6,1,96,128]{3,2,0,1:T(8,128)S(1)} collective-permute-done((f32[6,1,96,128]{3,2,0,1:T(8,128)S(1)}, f32[6,1,96,128]{3,2,0,1:T(8,128)S(1)}, u32[]{:S(2)}, u32[]{:S(2)}) %collective-permute-start) | collective-permute-done | bytes 294944 | tf_op jit(solution)/shard_map/ppermute | solution.py:12
  11.9 0.1 subtract_bitcast_fusion
  12.1 1.8 %collective-permute-start.1 = (f32[2,6,1,96,128]{4,3,1,2,0:T(8,128)S(1)}, f32[2,6,1,96,128]{4,3,1,2,0:T(8,128)S(1)}, u32[]{:S(2)}, u32[]{:S(2)}) collective-permute-start(f32[2,6,1,96,128]{4,3,1,2,0:T(8,128)S(1)} %maximum_select_fusion), channel_id=1, source_target_pairs={{0,8},{4,12},{8,0},{12,4},{16,24},{20,28},{24,16},{28,20},{1,9},{5... | collective-permute-start | bytes 1769480 | tf_op jit(solution)/shard_map/ppermute | solution.py:12
  14.0 12.6 %collective-permute-done.1 = f32[2,6,1,96,128]{4,3,1,2,0:T(8,128)S(1)} collective-permute-done((f32[2,6,1,96,128]{4,3,1,2,0:T(8,128)S(1)}, f32[2,6,1,96,128]{4,3,1,2,0:T(8,128)S(1)}, u32[]{:S(2)}, u32[]{:S(2)}) %collective-permute-start.1) | collective-permute-done | bytes 589856 | tf_op jit(solution)/shard_map/ppermute | solution.py:12
  26.6 0.1 multiply_subtract_fusion.1
  26.7 0.1 maximum_select_fusion.1
  27.0 0.3 fusion.31
  27.3 1.6 %collective-permute-done.2 = f32[2,6,1,96,128]{4,3,1,2,0:T(8,128)S(1)} collective-permute-done((f32[2,6,1,96,128]{4,3,1,2,0:T(8,128)S(1)}, f32[2,6,1,96,128]{4,3,1,2,0:T(8,128)S(1)}, u32[]{:S(2)}, u32[]{:S(2)}) %collective-permute-start.2) | collective-permute-done | bytes 589856 | tf_op jit(solution)/shard_map/ppermute | solution.py:12
  29.0 0.1 maximum_select_fusion.2
  29.2 0.6 fusion.8
  29.9 0.4 convolution_bitcast_fusion
  30.3 0.2 copy.25
  30.5 0.1 fusion.11
  30.6 3.6 %collective-permute-start.3 = (f32[3,1,96,1,64]{2,4,3,0,1:T(8,128)S(1)}, f32[3,1,96,1,64]{2,4,3,0,1:T(8,128)S(1)}, u32[]{:S(2)}, u32[]{:S(2)}) collective-permute-start(f32[3,1,96,1,64]{2,4,3,0,1:T(8,128)S(1)} %get-tuple-element.225), channel_id=1, source_target_pairs={{0,3},{1,0},{2,1},{3,2},{4,7},{5,4},{6,5},{7,6},{8,11},{9,8},{10,9... | collective-permute-start | bytes 221192 | tf_op jit(solution)/shard_map/ppermute | solution.py:121
  34.2 1.0 %collective-permute-start.5 = (f32[3,1,96,1,64]{2,4,3,0,1:T(8,128)S(1)}, f32[3,1,96,1,64]{2,4,3,0,1:T(8,128)S(1)}, u32[]{:S(2)}, u32[]{:S(2)}) collective-permute-start(f32[3,1,96,1,64]{2,4,3,0,1:T(8,128)S(1)} %get-tuple-element.223), channel_id=1, source_target_pairs={{0,1},{1,2},{2,3},{3,0},{4,5},{5,6},{6,7},{7,4},{8,9},{9,10},{10,1... | collective-permute-start | bytes 221192 | tf_op jit(solution)/shard_map/ppermute | solution.py:121
  35.2 16.9 %all_gather.6 = f32[384,96]{1,0:T(8,128)S(1)} all-gather(f32[96,96]{1,0:T(8,128)S(1)} %copy-done.2), channel_id=1, replica_groups=mesh['gx'=8,'gy'=4] {'gy'}, dimensions={0}, use_global_device_ids=true | all-gather | bytes 184320 | tf_op jit(solution)/shard_map/all_gather | solution.py:106
  52.1 13.6 %all_gather.7 = f32[384,96]{1,0:T(8,128)S(1)} all-gather(f32[96,96]{1,0:T(8,128)S(1)} %copy-done.3), channel_id=1, replica_groups=mesh['gx'=8,'gy'=4] {'gy'}, dimensions={0}, use_global_device_ids=true | all-gather | bytes 184320 | tf_op jit(solution)/shard_map/all_gather | solution.py:107
  65.7 0.3 concatenate.35
  66.0 0.1 constant_dynamic-slice_fusion.1
  66.2 0.3 reshape.108
  66.5 1.7 %while.30 = (s32[]{:T(128)}, f32[3,1,96,64]{2,3,0,1:T(8,128)S(1)}, f32[4,3,1,96,64]{3,4,1,2,0:T(8,128)S(1)}, f32[4,3,1,96,64]{3,0,4,1,2:T(4,128)S(1)}, f32[4,96,96]{2,1,0:T(8,128)S(1)}, /*index=5*/s32[]{:T(128)}, s32[]{:T(128)}) while((s32[]{:T(128)}, f32[3,1,96,64]{2,3,0,1:T(8,128)S(1)}, f32[4,3,1,96,64]{3,4,1,2,0:T(8,128)S(1)}, ...), condition=%wide.region_1.2_spmd.clone, body=%wide.region_0.1_spmd.clone.sunk | while | flops 21270532 | bytes 933987 | solution.py:53
  66.5 0.3 fusion.48
  66.8 0.1 constant_dynamic-slice_fusion.3
  66.9 0.3 fusion.48
  67.2 0.1 constant_dynamic-slice_fusion.3
  67.4 0.3 fusion.48
  67.6 0.1 constant_dynamic-slice_fusion.3
  67.8 0.3 fusion.48
  68.1 0.1 constant_dynamic-slice_fusion.3
  68.2 1.3 %while.31 = (s32[]{:T(128)}, f32[3,1,96,64]{2,3,0,1:T(8,128)S(1)}, f32[4,3,1,96,64]{3,4,1,2,0:T(8,128)S(1)}, f32[4,3,1,96,64]{3,4,1,2,0:T(8,128)S(1)}, f32[4,96,...) while((s32[]{:T(128)}, f32[3,1,96,64]{2,3,0,1:T(8,128)S(1)}, ...), condition=%wide.region_3.4_spmd.clone, body=%wide.region_2.3_spmd.clone.sunk | while | flops 21270532 | bytes 786547 | solution.py:54
  68.3 0.2 fusion.51
  68.6 0.3 fusion.51
  68.9 0.2 fusion.51
  69.3 0.3 fusion.51
  69.6 0.3 copy.32
  69.9 0.7 reshape.121
  70.6 0.5 broadcast.112
  71.2 2.6 %reduce = f32[384,3,64]{2,1,0:T(4,128)S(1)} reduce(f32[384,3,1,1,64]{4,3,2,1,0:T(1,128)S(1)} %bitcast.124, f32[]{:T(128)} %broadcast.112), dimensions={2,3}, to_apply=%bitcast.90.reduce_sub_computation | reduce | bytes 589828
  73.7 0.6 reshape.122
  74.3 10.3 %all_to_all.15 = f32[4,1,18432]{2,1,0:T(1,128)S(1)} all-to-all(f32[4,1,18432]{2,1,0:T(1,128)S(1)} %reshape.122), channel_id=1, replica_groups=mesh['gx'=8,'gy'=4] {'gy'}, dimensions={0} | all-to-all | bytes 589824 | tf_op jit(solution)/shard_map/all_to_all | solution.py:134
  84.6 1.5 %reduce.1 = f32[4,18432]{1,0:T(4,128)S(1)} reduce(f32[4,1,18432]{2,1,0:T(1,128)S(1)} %all_to_all.15, f32[]{:T(128)} %broadcast.112), dimensions={1}, to_apply=%all_to_all.11.reduce_sub_computation | reduce | bytes 589828 | tf_op jit(solution)/shard_map/all_to_all | solution.py:134
  86.1 0.7 reshape.123
  86.8 0.8 copy.29
  87.6 0.3 all_to_all.12
  87.9 0.9 copy.31
  (42 shorter events, 0.7 us)
Async XLA Ops:
  0.0 29.9 %copy-start = (f32[96,96]{1,0:T(8,128)S(1)}, f32[96,96]{1,0:T(8,128)}, u32[]{:S(2)}) copy-start(f32[96,96]{1,0:T(8,128)} %param.9) | copy-start | bytes 110596
  0.8 1.0 %copy-start.1 = (f32[3,1,96,128]{3,2,1,0:T(8,128)S(1)}, f32[3,1,96,128]{3,2,1,0:T(8,128)}, u32[]{:S(2)}) copy-start(f32[3,1,96,128]{3,2,1,0:T(8,128)} %param.8) | copy-start | bytes 442372
  1.9 10.1 %collective-permute-start = (f32[6,1,96,128]{3,2,0,1:T(8,128)S(1)}, f32[6,1,96,128]{3,2,0,1:T(8,128)S(1)}, u32[]{:S(2)}, u32[]{:S(2)}) collective-permute-start(f32[6,1,96,128]{3,2,0,1:T(8,128)S(1)} %pad_maximum_fusion), channel_id=1, source_target_pairs={{0,16},{4,20},{8,24},{12,28},{16,0},{20,4},{24,8},{28,12},{1,17},{... | collective-permute-start | bytes 884744 | tf_op jit(solution)/shard_map/ppermute | solution.py:12
  12.1 14.6 %collective-permute-start.1 = (f32[2,6,1,96,128]{4,3,1,2,0:T(8,128)S(1)}, f32[2,6,1,96,128]{4,3,1,2,0:T(8,128)S(1)}, u32[]{:S(2)}, u32[]{:S(2)}) collective-permute-start(f32[2,6,1,96,128]{4,3,1,2,0:T(8,128)S(1)} %maximum_select_fusion), channel_id=1, source_target_pairs={{0,8},{4,12},{8,0},{12,4},{16,24},{20,28},{24,16},{28,20},{1,9},{5... | collective-permute-start | bytes 1769480 | tf_op jit(solution)/shard_map/ppermute | solution.py:12
  26.9 2.1 %collective-permute-start.2 = (f32[2,6,1,96,128]{4,3,1,2,0:T(8,128)S(1)}, f32[2,6,1,96,128]{4,3,1,2,0:T(8,128)S(1)}, u32[]{:S(2)}, u32[]{:S(2)}) collective-permute-start(f32[2,6,1,96,128]{4,3,1,2,0:T(8,128)S(1)} %maximum_select_fusion.1), channel_id=1, source_target_pairs={{0,4},{4,0},{8,12},{12,8},{16,20},{20,16},{24,28},{28,24},{1,5},{5... | collective-permute-start | bytes 1769480 | tf_op jit(solution)/shard_map/ppermute | solution.py:12
  30.6 4.7 %copy-start.2 = (f32[96,96]{1,0:T(8,128)S(1)}, f32[96,96]{1,0:T(8,128)}, u32[]{:S(2)}) copy-start(f32[96,96]{1,0:T(8,128)} %param.10) | copy-start | bytes 110596
  30.6 35.1 %collective-permute-start.3 = (f32[3,1,96,1,64]{2,4,3,0,1:T(8,128)S(1)}, f32[3,1,96,1,64]{2,4,3,0,1:T(8,128)S(1)}, u32[]{:S(2)}, u32[]{:S(2)}) collective-permute-start(f32[3,1,96,1,64]{2,4,3,0,1:T(8,128)S(1)} %get-tuple-element.225), channel_id=1, source_target_pairs={{0,3},{1,0},{2,1},{3,2},{4,7},{5,4},{6,5},{7,6},{8,11},{9,8},{10,9... | collective-permute-start | bytes 221192 | tf_op jit(solution)/shard_map/ppermute | solution.py:121
  34.2 31.5 %collective-permute-start.4 = (f32[3,1,96,1,64]{2,4,3,0,1:T(8,128)S(1)}, f32[3,1,96,1,64]{2,4,3,0,1:T(8,128)S(1)}, u32[]{:S(2)}, u32[]{:S(2)}) collective-permute-start(f32[3,1,96,1,64]{2,4,3,0,1:T(8,128)S(1)} %get-tuple-element.224), channel_id=1, source_target_pairs={{0,2},{1,3},{2,0},{3,1},{4,6},{5,7},{6,4},{7,5},{8,10},{9,11},{10,... | collective-permute-start | bytes 221192 | tf_op jit(solution)/shard_map/ppermute | solution.py:121
  34.2 31.5 %collective-permute-start.5 = (f32[3,1,96,1,64]{2,4,3,0,1:T(8,128)S(1)}, f32[3,1,96,1,64]{2,4,3,0,1:T(8,128)S(1)}, u32[]{:S(2)}, u32[]{:S(2)}) collective-permute-start(f32[3,1,96,1,64]{2,4,3,0,1:T(8,128)S(1)} %get-tuple-element.223), channel_id=1, source_target_pairs={{0,1},{1,2},{2,3},{3,0},{4,5},{5,6},{6,7},{7,4},{8,9},{9,10},{10,1... | collective-permute-start | bytes 221192 | tf_op jit(solution)/shard_map/ppermute | solution.py:121
  35.2 16.9 %copy-start.3 = (f32[96,96]{1,0:T(8,128)S(1)}, f32[96,96]{1,0:T(8,128)}, u32[]{:S(2)}) copy-start(f32[96,96]{1,0:T(8,128)} %param.11) | copy-start | bytes 110596
